TPU v7x, 256 devices: a whole 4x4x8 slice. The times are simulated.
256 devices in a mesh: seq: 32 (over x, z), ch: 8 (over y, core).
Axes of the slice: x: 4, y: 4, z: 8, core: 2. Of those that a mesh axis runs over, the one named last changes fastest.
Arguments:
- query_rows: float32 [16384, 2048], P('seq', 'ch'), may hold values from -6 to 6
- key_rows: float32 [16384, 2048], P('seq', 'ch'), may hold values from -6 to 6
- value_rows: float32 [16384, 2048], P('seq', 'ch'), may hold values from -6 to 6
- filters: float32 [16384, 2048], P('seq', 'ch'), may hold values from -0.046875 to 0.046875
- skip_gain: float32 [2048], P('ch'), may hold values from -4 to 4
- out_weight: float32 [2048, 2048], P('ch'), may hold values from -0.125 to 0.125
Outputs:
- projected: float32 [2048, 16384], P('ch', 'seq')
All inputs are finite; a program needn't handle non-finite values.
Results may differ from a plain program's by a relative error of at most 0.00007.
Values sent between devices are 32-bit elements; how exact they have to be, the bound alone decides.
A program may use at most 64 MiB of HBM per device.

v0:
```python
import functools
import math

import jax
import jax.numpy as jnp
import numpy as np
from jax import lax
from jax.experimental import pallas as pl
from jax.experimental.pallas import tpu as pltpu
from jax.sharding import PartitionSpec as P

CHUNKS = 2
LANES = 128
MESH = pl.DeviceIdType.MESH


def split_table(table):
    high = table.astype(jnp.bfloat16)
    low = (table - high.astype(np.float64)).astype(jnp.bfloat16)
    return high, low


def tables(parts, per_part):
    rows = parts * per_part
    period = 2 * rows * LANES
    odd = np.arange(rows) + 0.5
    outer = 2 * math.pi * odd[:, None] * np.arange(rows)[None, :] / (2 * rows)
    first = np.zeros((2, 2, rows, parts, 2, per_part))
    for pair in range(2):
        first[0, pair, :, :, pair, :] = np.cos(outer).reshape(rows, parts, per_part)
        first[1, pair, :, :, pair, :] = -np.sin(outer).reshape(rows, parts, per_part)
    first = first.reshape(4 * rows, 2 * rows)
    last = first.T * (2.0 / period)
    turn = 2 * math.pi * odd[:, None] * np.arange(LANES)[None, :] / period
    turn_cos = np.tile(np.cos(turn), (2, 2)).astype(np.float32)
    turn_sin = np.tile(np.sin(turn), (2, 2)).astype(np.float32)
    inner = 2 * math.pi * (np.arange(LANES)[:, None] * np.arange(LANES)[None, :] % LANES) / LANES
    cos, sin = np.cos(inner), np.sin(inner)
    ahead = np.block([[cos, -sin], [sin, cos]])
    behind = np.block([[cos, sin], [-sin, cos]])
    return (
        *split_table(first),
        *split_table(last),
        *split_table(ahead),
        *split_table(behind),
        turn_cos,
        turn_sin,
    )


def split(value):
    high = value.astype(jnp.bfloat16)
    low = (value - high.astype(jnp.float32)).astype(jnp.bfloat16)
    return high, low


def dot(a, b):
    return jnp.dot(a, b, preferred_element_type=jnp.float32)


def dot3(a, b):
    return dot(a[0], b[0]) + dot(a[0], b[1]) + dot(a[1], b[0])


def convolve_pair(data, first, last, ahead, behind, turn_cos, turn_sin):
    half = data.shape[0]
    stage = dot3(first, split(data))
    re, im = stage[:half], stage[half:]
    cos, sin = turn_cos[...], turn_sin[...]
    re, im = re * cos + im * sin, im * cos - re * sin
    stage = jnp.concatenate(
        [
            jnp.concatenate([re[:, :LANES], im[:, :LANES]], axis=1),
            jnp.concatenate([re[:, LANES:], im[:, LANES:]], axis=1),
        ],
        axis=0,
    )
    stage = dot3(split(stage), ahead)
    gre, gim = stage[:half, :LANES], stage[:half, LANES:]
    fre, fim = stage[half:, :LANES], stage[half:, LANES:]
    stage = jnp.concatenate([gre * fre - gim * fim, gre * fim + gim * fre], axis=1)
    stage = dot3(split(stage), behind)
    re, im = stage[:, :LANES], stage[:, LANES:]
    cos, sin = cos[:, :LANES], sin[:, :LANES]
    stage = jnp.concatenate([re * cos - im * sin, im * cos + re * sin], axis=0)
    return dot3(last, split(stage))


def kernel(
    parts,
    ys,
    query_hbm,
    key_hbm,
    value_hbm,
    filter_hbm,
    skip_hbm,
    weight_hbm,
    *rest,
):
    table_hbm, rest = rest[:10], rest[10:]
    out_ref, rest = rest[0], rest[1:]
    table_ref, rest = rest[:10], rest[10:]
    (
        query_in,
        key_in,
        value_in,
        filter_in,
        skip_in,
        query_t,
        sent,
        got,
        conv_sent,
        conv_got,
        weights,
        weight_t,
        mixed,
        total,
        partner_got,
        load_sem,
        table_sem,
        send_sem,
        recv_sem,
        conv_send_sem,
        conv_recv_sem,
        weight_send_sem,
        weight_recv_sem,
        mixed_send_sem,
        mixed_recv_sem,
        partner_send_sem,
        partner_recv_sem,
    ) = rest
    length, channels = query_in.shape
    per_part = length // LANES
    chunk_channels = channels // CHUNKS
    slab = chunk_channels // parts * per_part
    outs = weights.shape[2]
    me = lax.axis_index("seq")
    lane = lax.axis_index("ch")
    core = lax.rem(lane, 2)
    own_y = lane // 2
    partner = lane + 1 - 2 * core
    own_half = pl.multiple_of(core * (outs // 2), outs // 2)
    partner_half = pl.multiple_of((1 - core) * (outs // 2), outs // 2)

    loads = [
        pltpu.make_async_copy(source, target, load_sem.at[number])
        for number, (source, target) in enumerate(
            [
                (filter_hbm, filter_in),
                (skip_hbm, skip_in),
                (key_hbm, key_in),
                (value_hbm, value_in),
                (query_hbm, query_in),
            ]
        )
    ]
    for load in loads[:4]:
        load.start()

    barrier = pltpu.get_barrier_semaphore()

    @pl.loop(1, parts)
    def _(step):
        pl.semaphore_signal(
            barrier, inc=1, device_id={"seq": lax.rem(me + step, parts)}, device_id_type=MESH
        )

    @pl.loop(1, ys)
    def _(step):
        pl.semaphore_signal(
            barrier, inc=1, device_id={"ch": lax.rem(lane + 2 * step, 2 * ys)}, device_id_type=MESH
        )

    pl.semaphore_signal(barrier, inc=1, device_id={"ch": partner}, device_id_type=MESH)

    loads[4].start()
    table_loads = [
        pltpu.make_async_copy(source, target, table_sem.at[number])
        for number, (source, target) in enumerate(zip(table_hbm, table_ref))
    ]
    for load in table_loads:
        load.start()

    def place(source, which, columns):
        for row in range(per_part):
            block = source(pl.ds(row * LANES, LANES), pl.ds(columns, LANES))
            sent[which, pl.ds(columns * per_part + row, LANES, stride=per_part), :] = block.T

    for load in loads[:4]:
        load.wait()
    tap = jnp.where(me == 0, 1.0, 0.0).astype(jnp.float32)
    filter_in[0:1, :] = filter_in[0:1, :] + tap * skip_in[...]

    def send_chunk(chunk):
        for which in range(2):

            @pl.loop(1, parts)
            def _(step):
                peer = lax.rem(me + step, parts)
                start = pl.multiple_of(chunk * parts * slab + peer * slab, slab)
                pltpu.make_async_remote_copy(
                    src_ref=sent.at[which, pl.ds(start, slab), :],
                    dst_ref=got.at[which, chunk, me],
                    send_sem=send_sem.at[which, chunk],
                    recv_sem=recv_sem.at[which, chunk],
                    device_id={"seq": peer},
                    device_id_type=MESH,
                ).start()

            start = pl.multiple_of(chunk * parts * slab + me * slab, slab)
            pltpu.make_async_copy(
                sent.at[which, pl.ds(start, slab), :],
                got.at[which, chunk, me],
                recv_sem.at[which, chunk],
            ).start()

    def gated(rows, columns):
        return key_in[rows, columns] * value_in[rows, columns]

    def plain(rows, columns):
        return filter_in[rows, columns]

    sent_chunks = 0
    for columns in range(0, channels, LANES):
        place(plain, 1, columns)
        place(gated, 0, columns)
        if columns == 0:
            pl.semaphore_wait(barrier, parts - 1 + ys - 1 + 1)
        while (sent_chunks + 1) * chunk_channels <= columns + LANES:
            send_chunk(sent_chunks)
            sent_chunks += 1

    def weight_copy(step):
        peer_y = lax.rem(own_y + step, ys)
        start = pl.multiple_of(peer_y * outs, outs)
        return pltpu.make_async_remote_copy(
            src_ref=weight_hbm.at[:, pl.ds(start, outs)],
            dst_ref=weights.at[own_y],
            send_sem=weight_send_sem.at[step - 1],
            recv_sem=weight_recv_sem.at[step - 1],
            device_id={"ch": lax.rem(lane + 2 * step, 2 * ys)},
            device_id_type=MESH,
        )

    for step in range(1, ys):
        weight_copy(step).start()
    own_weight = pltpu.make_async_copy(
        weight_hbm.at[:, pl.ds(pl.multiple_of(own_y * outs, outs), outs)],
        weights.at[own_y],
        weight_recv_sem.at[ys - 1],
    )
    own_weight.start()

    loads[4].wait()
    for columns in range(0, channels, LANES):
        for row in range(per_part):
            query_t[pl.ds(columns, LANES), pl.ds(row * LANES, LANES)] = query_in[
                pl.ds(row * LANES, LANES), pl.ds(columns, LANES)
            ].T
    for load in table_loads:
        load.wait()

    first, last, ahead, behind = (
        (table_ref[2 * n][...], table_ref[2 * n + 1][...]) for n in range(4)
    )
    turn_cos, turn_sin = table_ref[8], table_ref[9]

    @pl.loop(0, CHUNKS)
    def _(chunk):
        for which in range(2):
            pltpu.make_async_copy(
                got.at[which, chunk], got.at[which, chunk], recv_sem.at[which, chunk]
            ).wait()

        @pl.loop(0, slab // 8)
        def _(pair):
            rows = pl.ds(pl.multiple_of(pair * 8, 8), 8)
            data = jnp.concatenate(
                [got[which, chunk, :, rows, :].reshape(parts * 8, LANES) for which in range(2)],
                axis=1,
            )
            done = convolve_pair(data, first, last, ahead, behind, turn_cos, turn_sin)
            conv_sent[chunk, :, rows, :] = done.reshape(parts, 8, LANES)

        place_at = pl.ds(pl.multiple_of(me * slab, slab), slab)

        @pl.loop(1, parts)
        def _(step):
            peer = lax.rem(me + step, parts)
            pltpu.make_async_remote_copy(
                src_ref=conv_sent.at[chunk, peer],
                dst_ref=conv_got.at[chunk, place_at, :],
                send_sem=conv_send_sem.at[chunk],
                recv_sem=conv_recv_sem.at[chunk],
                device_id={"seq": peer},
                device_id_type=MESH,
            ).start()

        pltpu.make_async_copy(
            conv_sent.at[chunk, me], conv_got.at[chunk, place_at, :], conv_recv_sem.at[chunk]
        ).start()

    own_weight.wait()
    for step in range(1, ys):
        weight_copy(step).wait_recv()

    @pl.loop(0, ys)
    def _(y):
        for chunk in range(CHUNKS):
            for out in range(0, outs, LANES):
                block = weights[y, pl.ds(chunk * chunk_channels, chunk_channels), pl.ds(out, LANES)].T
                high, low = split(block)
                weight_t[y, chunk, pl.ds(out, LANES), :] = jnp.concatenate([high, low, high], axis=1)

    total[...] = jnp.zeros_like(total)

    def mixed_copy(chunk, step):
        return pltpu.make_async_remote_copy(
            src_ref=mixed.at[own_y, chunk],
            dst_ref=mixed.at[own_y, chunk],
            send_sem=mixed_send_sem.at[chunk, step - 1],
            recv_sem=mixed_recv_sem.at[chunk, step - 1],
            device_id={"ch": lax.rem(lane + 2 * step, 2 * ys)},
            device_id_type=MESH,
        )

    def project(y, chunk):
        high, low = split(mixed[y, chunk])
        data = jnp.concatenate([high, high, low], axis=0)
        total[...] += dot(weight_t[y, chunk], data)

    @pl.loop(0, CHUNKS)
    def _(chunk):
        pltpu.make_async_copy(
            conv_got.at[chunk], conv_got.at[chunk], conv_recv_sem.at[chunk]
        ).wait()
        rows = pl.ds(pl.multiple_of(chunk * chunk_channels, chunk_channels), chunk_channels)
        for row in range(per_part):
            columns = pl.ds(row * LANES, LANES)
            mixed[own_y, chunk, :, columns] = (
                conv_got[chunk, pl.ds(row, chunk_channels, stride=per_part), :]
                * query_t[rows, columns]
            )
        for step in range(1, ys):
            mixed_copy(chunk, step).start()
        project(own_y, chunk)

    @pl.loop(0, CHUNKS)
    def _(chunk):
        for step in range(1, ys):
            mixed_copy(chunk, step).wait_recv()
            project(lax.rem(own_y + ys - step, ys), chunk)

    to_partner = pltpu.make_async_remote_copy(
        src_ref=total.at[pl.ds(partner_half, outs // 2), :],
        dst_ref=partner_got,
        send_sem=partner_send_sem,
        recv_sem=partner_recv_sem,
        device_id={"ch": partner},
        device_id_type=MESH,
    )
    to_partner.start()

    @pl.loop(0, CHUNKS)
    def _(chunk):
        for which in range(2):
            rest_of = got.at[which, chunk, pl.ds(0, parts - 1)]
            pltpu.make_async_copy(rest_of, rest_of, send_sem.at[which, chunk]).wait()
        rest_of = conv_sent.at[chunk, pl.ds(0, parts - 1)]
        pltpu.make_async_copy(rest_of, rest_of, conv_send_sem.at[chunk]).wait()
        for step in range(1, ys):
            mixed_copy(chunk, step).wait_send()

    for step in range(1, ys):
        weight_copy(step).wait_send()
    to_partner.wait()
    out_ref[...] = total[pl.ds(own_half, outs // 2), :] + partner_got[...]


def per_device(query_rows, key_rows, value_rows, filters, skip_gain, out_weight):
    parts = lax.axis_size("seq")
    ys = lax.axis_size("ch") // 2
    length, channels = query_rows.shape
    per_part = length // LANES
    outs = out_weight.shape[1] // ys
    chunk_channels = channels // CHUNKS
    slab = chunk_channels // parts * per_part
    consts = tables(parts, per_part)
    f32 = jnp.float32
    dma = pltpu.SemaphoreType.DMA
    return pl.pallas_call(
        functools.partial(kernel, parts, ys),
        out_shape=jax.ShapeDtypeStruct((outs // 2, length), f32),
        in_specs=[pl.BlockSpec(memory_space=pl.ANY)] * (6 + len(consts)),
        out_specs=pl.BlockSpec(memory_space=pltpu.VMEM),
        scratch_shapes=[
            *[pltpu.VMEM(table.shape, table.dtype) for table in consts],
            pltpu.VMEM((length, channels), f32),
            pltpu.VMEM((length, channels), f32),
            pltpu.VMEM((length, channels), f32),
            pltpu.VMEM((length, channels), f32),
            pltpu.VMEM((1, channels), f32),
            pltpu.VMEM((channels, length), f32),
            pltpu.VMEM((2, channels * per_part, LANES), f32),
            pltpu.VMEM((2, CHUNKS, parts, slab, LANES), f32),
            pltpu.VMEM((CHUNKS, parts, slab, LANES), f32),
            pltpu.VMEM((CHUNKS, parts * slab, LANES), f32),
            pltpu.VMEM((ys, channels, outs), f32),
            pltpu.VMEM((ys, CHUNKS, outs, 3 * chunk_channels), jnp.bfloat16),
            pltpu.VMEM((ys, CHUNKS, chunk_channels, length), f32),
            pltpu.VMEM((outs, length), f32),
            pltpu.VMEM((outs // 2, length), f32),
            dma((5,)),
            dma((len(consts),)),
            dma((2, CHUNKS)),
            dma((2, CHUNKS)),
            dma((CHUNKS,)),
            dma((CHUNKS,)),
            dma((ys - 1,)),
            dma((ys,)),
            dma((CHUNKS, ys - 1)),
            dma((CHUNKS, ys - 1)),
            dma(()),
            dma(()),
        ],
        compiler_params=pltpu.CompilerParams(collective_id=0, has_side_effects=True),
    )(
        query_rows,
        key_rows,
        value_rows,
        filters,
        skip_gain.reshape(1, channels),
        out_weight,
        *[jnp.asarray(table) for table in consts],
    )


def solution(mesh):
    in_specs = (
        P("seq", "ch"),
        P("seq", "ch"),
        P("seq", "ch"),
        P("seq", "ch"),
        P("ch"),
        P("ch", None),
    )
    out_specs = P("ch", "seq")
    return jax.shard_map(
        per_device, mesh=mesh, in_specs=in_specs, out_specs=out_specs, check_vma=False
    )
```

profile of v0, /device:TPU:1, one launch (start us, length us, event | category | flops | bytes accessed | tf_op | source)
XLA Modules:
  0.0 71.9 jit_solution(16738005316790055346)
XLA Ops:
  0.0 70.1 %shard_map.154 = f32[256,512]{1,0:T(8,128)} custom-call(f32[512,256]{1,0:T(8,128)} %query_hbm.1, f32[512,256]{1,0:T(8,128)} %key_hbm.1, f32[512,256]{1,0:T(8,128)} %value_hbm.1, f32[512,256]{1,0:T(8,128)} %filter_hbm.1, f32[1,256]{1,0:T(1,128)} %bitcast.1, f32[256,2048]{1,0:T(8,128)} %weight_hbm.1, bf16[512,256]{1,0:T(8,128)(2,1)} %constant.20.clone.rest_0_, ...), custom_call_target="tpu_custom_call" | custom-call | tf_op jit(solution)/shard_map/pallas_call | solution.py:391
  70.1 1.9 %copy.18 = f32[256,512]{1,0:T(8,128)} copy(f32[256,512]{1,0:T(8,128)} %shard_map.154) | data formatting | bytes 1048576
where the time goes:
time: 72.1 us; the launch traced here: 71.9 us
  Pallas kernels  70.1 us (97%)
  local copies, waits for them, and re-layouts  1.87 us (3%)
    pallas_call x1, Pallas kernels, per_device(): pl.pallas_call(functools.partial(kernel, parts, ys), out_shape=jax.ShapeD...  70.1 us
    unnamed x1, local copies, waits for them, and re-layouts  1.87 us

commit v1 on v0

--- a/solution.py
+++ b/solution.py
@@ -9,7 +9,9 @@
 from jax.experimental.pallas import tpu as pltpu
 from jax.sharding import PartitionSpec as P
 
-CHUNKS = 2
+CHUNKS = 4
+HELD = 1
+LAG = CHUNKS - 1 - HELD
 LANES = 128
 MESH = pl.DeviceIdType.MESH
 
@@ -220,16 +222,6 @@
     def plain(rows, columns):
         return filter_in[rows, columns]
 
-    sent_chunks = 0
-    for columns in range(0, channels, LANES):
-        place(plain, 1, columns)
-        place(gated, 0, columns)
-        if columns == 0:
-            pl.semaphore_wait(barrier, parts - 1 + ys - 1 + 1)
-        while (sent_chunks + 1) * chunk_channels <= columns + LANES:
-            send_chunk(sent_chunks)
-            sent_chunks += 1
-
     def weight_copy(step):
         peer_y = lax.rem(own_y + step, ys)
         start = pl.multiple_of(peer_y * outs, outs)
@@ -242,14 +234,24 @@
             device_id_type=MESH,
         )
 
-    for step in range(1, ys):
-        weight_copy(step).start()
     own_weight = pltpu.make_async_copy(
         weight_hbm.at[:, pl.ds(pl.multiple_of(own_y * outs, outs), outs)],
         weights.at[own_y],
         weight_recv_sem.at[ys - 1],
     )
-    own_weight.start()
+    sent_chunks = 0
+    for columns in range(0, channels, LANES):
+        place(plain, 1, columns)
+        place(gated, 0, columns)
+        if columns == 0:
+            pl.semaphore_wait(barrier, parts - 1 + ys - 1 + 1)
+            for step in range(1, ys):
+                weight_copy(step).start()
+            own_weight.start()
+        while (sent_chunks + 1) * chunk_channels <= columns + LANES:
+            if sent_chunks < CHUNKS - HELD:
+                send_chunk(sent_chunks)
+            sent_chunks += 1
 
     loads[4].wait()
     for columns in range(0, channels, LANES):
@@ -265,8 +267,20 @@
     )
     turn_cos, turn_sin = table_ref[8], table_ref[9]
 
-    @pl.loop(0, CHUNKS)
-    def _(chunk):
+    def prepare_weights():
+        own_weight.wait()
+        for step in range(1, ys):
+            weight_copy(step).wait_recv()
+
+        @pl.loop(0, ys)
+        def _(y):
+            for chunk in range(CHUNKS):
+                for out in range(0, outs, LANES):
+                    block = weights[y, pl.ds(chunk * chunk_channels, chunk_channels), pl.ds(out, LANES)].T
+                    high, low = split(block)
+                    weight_t[y, chunk, pl.ds(out, LANES), :] = jnp.concatenate([high, low, high], axis=1)
+
+    def convolve_chunk(chunk):
         for which in range(2):
             pltpu.make_async_copy(
                 got.at[which, chunk], got.at[which, chunk], recv_sem.at[which, chunk]
@@ -300,56 +314,107 @@
             conv_sent.at[chunk, me], conv_got.at[chunk, place_at, :], conv_recv_sem.at[chunk]
         ).start()
 
-    own_weight.wait()
-    for step in range(1, ys):
-        weight_copy(step).wait_recv()
-
-    @pl.loop(0, ys)
-    def _(y):
-        for chunk in range(CHUNKS):
-            for out in range(0, outs, LANES):
-                block = weights[y, pl.ds(chunk * chunk_channels, chunk_channels), pl.ds(out, LANES)].T
-                high, low = split(block)
-                weight_t[y, chunk, pl.ds(out, LANES), :] = jnp.concatenate([high, low, high], axis=1)
+        @pl.when(chunk < HELD)
+        def _():
+            send_chunk(chunk + CHUNKS - HELD)
 
     total[...] = jnp.zeros_like(total)
 
-    def mixed_copy(chunk, step):
+    ahead_y, behind_y = lax.rem(own_y + 1, ys), lax.rem(own_y + ys - 1, ys)
+    across_y = lax.rem(own_y + 2, ys)
+    half_rows = chunk_channels // 2
+
+    def mixed_copy(chunk, owner, half, up, slot):
         return pltpu.make_async_remote_copy(
-            src_ref=mixed.at[own_y, chunk],
-            dst_ref=mixed.at[own_y, chunk],
-            send_sem=mixed_send_sem.at[chunk, step - 1],
-            recv_sem=mixed_recv_sem.at[chunk, step - 1],
-            device_id={"ch": lax.rem(lane + 2 * step, 2 * ys)},
+            src_ref=mixed.at[owner, chunk, pl.ds(half * half_rows, half_rows), :],
+            dst_ref=mixed.at[owner, chunk, pl.ds(half * half_rows, half_rows), :],
+            send_sem=mixed_send_sem.at[chunk, slot],
+            recv_sem=mixed_recv_sem.at[chunk, slot],
+            device_id={"ch": lax.rem(lane + (2 if up else 2 * ys - 2), 2 * ys)},
             device_id_type=MESH,
         )
+
+    def own_copies(chunk):
+        return [
+            mixed_copy(chunk, own_y, 0, True, 0),
+            mixed_copy(chunk, own_y, 1, False, 1),
+            mixed_copy(chunk, own_y, 1, True, 2),
+            mixed_copy(chunk, own_y, 0, False, 3),
+        ]
+
+    def relay_copies(chunk):
+        return [
+            mixed_copy(chunk, behind_y, 0, True, 4),
+            mixed_copy(chunk, ahead_y, 1, False, 5),
+        ]
 
     def project(y, chunk):
         high, low = split(mixed[y, chunk])
         data = jnp.concatenate([high, high, low], axis=0)
         total[...] += dot(weight_t[y, chunk], data)
 
-    @pl.loop(0, CHUNKS)
-    def _(chunk):
+    def relay(chunk):
+        mixed_copy(chunk, own_y, 0, True, 0).wait_recv()
+        mixed_copy(chunk, behind_y, 0, True, 4).start()
+        mixed_copy(chunk, own_y, 1, False, 1).wait_recv()
+        mixed_copy(chunk, ahead_y, 1, False, 5).start()
+
+    def finish(chunk):
+        mixed_copy(chunk, own_y, 1, True, 2).wait_recv()
+        project(behind_y, chunk)
+        mixed_copy(chunk, own_y, 0, False, 3).wait_recv()
+        project(ahead_y, chunk)
+        for copy in relay_copies(chunk):
+            copy.wait_recv()
+        project(across_y, chunk)
+
+    def gather(chunk):
         pltpu.make_async_copy(
             conv_got.at[chunk], conv_got.at[chunk], conv_recv_sem.at[chunk]
         ).wait()
-        rows = pl.ds(pl.multiple_of(chunk * chunk_channels, chunk_channels), chunk_channels)
         for row in range(per_part):
+            rows = pl.ds(pl.multiple_of(chunk * chunk_channels, chunk_channels), chunk_channels)
             columns = pl.ds(row * LANES, LANES)
             mixed[own_y, chunk, :, columns] = (
                 conv_got[chunk, pl.ds(row, chunk_channels, stride=per_part), :]
                 * query_t[rows, columns]
             )
-        for step in range(1, ys):
-            mixed_copy(chunk, step).start()
-        project(own_y, chunk)
-
-    @pl.loop(0, CHUNKS)
-    def _(chunk):
-        for step in range(1, ys):
-            mixed_copy(chunk, step).wait_recv()
-            project(lax.rem(own_y + ys - step, ys), chunk)
+        for copy in own_copies(chunk):
+            copy.start()
+
+    @pl.loop(0, CHUNKS + LAG)
+    def _(step):
+        @pl.when(step < CHUNKS)
+        def _():
+            convolve_chunk(step)
+
+        @pl.when((step < CHUNKS) & (step > LAG))
+        def _():
+            relay(step - LAG - 1)
+
+        @pl.when(step >= LAG)
+        def _():
+            gather(step - LAG)
+
+        @pl.when(step == LAG)
+        def _():
+            prepare_weights()
+
+        @pl.when((step >= CHUNKS) & (step > LAG))
+        def _():
+            relay(step - LAG - 1)
+
+        @pl.when(step >= LAG)
+        def _():
+            project(own_y, step - LAG)
+
+        @pl.when(step > LAG + 1)
+        def _():
+            finish(step - LAG - 2)
+
+    relay(CHUNKS - 1)
+    finish(CHUNKS - 2)
+    finish(CHUNKS - 1)
 
     to_partner = pltpu.make_async_remote_copy(
         src_ref=total.at[pl.ds(partner_half, outs // 2), :],
@@ -368,8 +433,8 @@
             pltpu.make_async_copy(rest_of, rest_of, send_sem.at[which, chunk]).wait()
         rest_of = conv_sent.at[chunk, pl.ds(0, parts - 1)]
         pltpu.make_async_copy(rest_of, rest_of, conv_send_sem.at[chunk]).wait()
-        for step in range(1, ys):
-            mixed_copy(chunk, step).wait_send()
+        for copy in own_copies(chunk) + relay_copies(chunk):
+            copy.wait_send()
 
     for step in range(1, ys):
         weight_copy(step).wait_send()
@@ -390,7 +455,7 @@
     dma = pltpu.SemaphoreType.DMA
     return pl.pallas_call(
         functools.partial(kernel, parts, ys),
-        out_shape=jax.ShapeDtypeStruct((outs // 2, length), f32),
+        out_shape=pltpu.VMEM((outs // 2, length), f32),
         in_specs=[pl.BlockSpec(memory_space=pl.ANY)] * (6 + len(consts)),
         out_specs=pl.BlockSpec(memory_space=pltpu.VMEM),
         scratch_shapes=[
@@ -418,8 +483,8 @@
             dma((CHUNKS,)),
             dma((ys - 1,)),
             dma((ys,)),
-            dma((CHUNKS, ys - 1)),
-            dma((CHUNKS, ys - 1)),
+            dma((CHUNKS, 6)),
+            dma((CHUNKS, 6)),
             dma(()),
             dma(()),
         ],

time: 72.1 us -> 61.9 us (0.86)
  Pallas kernels: 70.1 us -> 61 us
  local copies, waits for them, and re-layouts: 1.87 us -> 0.8 us
    pallas_call x1, Pallas kernels: 70.1 us -> 61 us  [per_device(): pl.pallas_call(functools.partial(kernel, parts, ys), out_shape=pltpu.VMEM...]
    unnamed x1, local copies, waits for them, and re-layouts: 1.87 us -> 0.8 us
where the time goes in v1:
time: 61.9 us; the launch traced here: 61.8 us
  Pallas kernels  61 us (99%)
  local copies, waits for them, and re-layouts  0.8 us (1%)
    pallas_call x1, Pallas kernels, per_device(): pl.pallas_call(functools.partial(kernel, parts, ys), out_shape=pltpu.VMEM...  61 us

profile of v1, /device:TPU:1, one launch (start us, length us, event | category | flops | bytes accessed | tf_op | source)
XLA Modules:
  0.0 61.8 jit_solution(746684685103688687)
XLA Ops:
  0.0 61.0 %shard_map.154 = f32[256,512]{1,0:T(8,128)S(1)} custom-call(f32[512,256]{1,0:T(8,128)} %query_hbm.1, f32[512,256]{1,0:T(8,128)} %key_hbm.1, f32[512,256]{1,0:T(8,128)} %value_hbm.1, f32[512,256]{1,0:T(8,128)} %filter_hbm.1, f32[1,256]{1,0:T(1,128)} %bitcast.1, f32[256,2048]{1,0:T(8,128)} %weight_hbm.1, bf16[512,256]{1,0:T(8,128)(2,1)} %constant.20.clone.rest_0_, ...), custom_call_target="tpu_custom_call" | custom-call | tf_op jit(solution)/shard_map/pallas_call | solution.py:456
  61.0 0.8 %copy.18 = f32[256,512]{1,0:T(8,128)} copy(f32[256,512]{1,0:T(8,128)S(1)} %shard_map.154) | data formatting | bytes 1048576

commit v2 on v1

--- a/solution.py
+++ b/solution.py
@@ -34,8 +34,8 @@
     first = first.reshape(4 * rows, 2 * rows)
     last = first.T * (2.0 / period)
     turn = 2 * math.pi * odd[:, None] * np.arange(LANES)[None, :] / period
-    turn_cos = np.tile(np.cos(turn), (2, 2)).astype(np.float32)
-    turn_sin = np.tile(np.sin(turn), (2, 2)).astype(np.float32)
+    turn_cos = np.tile(np.cos(turn), (2, 1)).astype(np.float32)
+    turn_sin = np.tile(np.sin(turn), (2, 1)).astype(np.float32)
     inner = 2 * math.pi * (np.arange(LANES)[:, None] * np.arange(LANES)[None, :] % LANES) / LANES
     cos, sin = np.cos(inner), np.sin(inner)
     ahead = np.block([[cos, -sin], [sin, cos]])
@@ -64,28 +64,25 @@
     return dot(a[0], b[0]) + dot(a[0], b[1]) + dot(a[1], b[0])
 
 
-def convolve_pair(data, first, last, ahead, behind, turn_cos, turn_sin):
+def dot3_narrow(a, b):
+    width = b[0].shape[1]
+    both = dot(a[0], jnp.concatenate(b, axis=1))
+    return both[:, :width] + both[:, width:] + dot(a[1], b[0])
+
+
+def spectrum(data, first, ahead, cos, sin):
     half = data.shape[0]
-    stage = dot3(first, split(data))
+    stage = dot3_narrow(first, split(data))
     re, im = stage[:half], stage[half:]
-    cos, sin = turn_cos[...], turn_sin[...]
-    re, im = re * cos + im * sin, im * cos - re * sin
-    stage = jnp.concatenate(
-        [
-            jnp.concatenate([re[:, :LANES], im[:, :LANES]], axis=1),
-            jnp.concatenate([re[:, LANES:], im[:, LANES:]], axis=1),
-        ],
-        axis=0,
-    )
-    stage = dot3(split(stage), ahead)
-    gre, gim = stage[:half, :LANES], stage[:half, LANES:]
-    fre, fim = stage[half:, :LANES], stage[half:, LANES:]
-    stage = jnp.concatenate([gre * fre - gim * fim, gre * fim + gim * fre], axis=1)
-    stage = dot3(split(stage), behind)
+    stage = jnp.concatenate([re * cos + im * sin, im * cos - re * sin], axis=1)
+    return dot3(split(stage), ahead)
+
+
+def inverse(product, behind, last, cos, sin):
+    stage = dot3(split(product), behind)
     re, im = stage[:, :LANES], stage[:, LANES:]
-    cos, sin = cos[:, :LANES], sin[:, :LANES]
     stage = jnp.concatenate([re * cos - im * sin, im * cos + re * sin], axis=0)
-    return dot3(last, split(stage))
+    return dot3_narrow(last, split(stage))
 
 
 def kernel(
@@ -109,6 +106,7 @@
         filter_in,
         skip_in,
         query_t,
+        filter_spectrum,
         sent,
         got,
         conv_sent,
@@ -194,7 +192,7 @@
     filter_in[0:1, :] = filter_in[0:1, :] + tap * skip_in[...]
 
     def send_chunk(chunk):
-        for which in range(2):
+        for which in (1, 0):
 
             @pl.loop(1, parts)
             def _(step):
@@ -281,19 +279,32 @@
                     weight_t[y, chunk, pl.ds(out, LANES), :] = jnp.concatenate([high, low, high], axis=1)
 
     def convolve_chunk(chunk):
-        for which in range(2):
+        def arrived(which):
             pltpu.make_async_copy(
                 got.at[which, chunk], got.at[which, chunk], recv_sem.at[which, chunk]
             ).wait()
 
+        def transformed(which, rows):
+            data = got[which, chunk, :, rows, :].reshape(parts * 8, LANES)
+            return spectrum(data, first, ahead, turn_cos[...], turn_sin[...])
+
+        arrived(1)
+
         @pl.loop(0, slab // 8)
         def _(pair):
             rows = pl.ds(pl.multiple_of(pair * 8, 8), 8)
-            data = jnp.concatenate(
-                [got[which, chunk, :, rows, :].reshape(parts * 8, LANES) for which in range(2)],
-                axis=1,
-            )
-            done = convolve_pair(data, first, last, ahead, behind, turn_cos, turn_sin)
+            filter_spectrum[pair] = transformed(1, rows)
+
+        arrived(0)
+
+        @pl.loop(0, slab // 8)
+        def _(pair):
+            rows = pl.ds(pl.multiple_of(pair * 8, 8), 8)
+            stage = transformed(0, rows)
+            gre, gim = stage[:, :LANES], stage[:, LANES:]
+            fre, fim = filter_spectrum[pair, :, :LANES], filter_spectrum[pair, :, LANES:]
+            product = jnp.concatenate([gre * fre - gim * fim, gre * fim + gim * fre], axis=1)
+            done = inverse(product, behind, last, turn_cos[...], turn_sin[...])
             conv_sent[chunk, :, rows, :] = done.reshape(parts, 8, LANES)
 
         place_at = pl.ds(pl.multiple_of(me * slab, slab), slab)
@@ -359,14 +370,32 @@
         mixed_copy(chunk, own_y, 1, False, 1).wait_recv()
         mixed_copy(chunk, ahead_y, 1, False, 5).start()
 
-    def finish(chunk):
+    to_partner = pltpu.make_async_remote_copy(
+        src_ref=total.at[pl.ds(partner_half, outs // 2), :],
+        dst_ref=partner_got,
+        send_sem=partner_send_sem,
+        recv_sem=partner_recv_sem,
+        device_id={"ch": partner},
+        device_id_type=MESH,
+    )
+
+    def finish(chunk, final=False):
         mixed_copy(chunk, own_y, 1, True, 2).wait_recv()
         project(behind_y, chunk)
         mixed_copy(chunk, own_y, 0, False, 3).wait_recv()
         project(ahead_y, chunk)
         for copy in relay_copies(chunk):
             copy.wait_recv()
-        project(across_y, chunk)
+        if not final:
+            project(across_y, chunk)
+            return
+        high, low = split(mixed[across_y, chunk])
+        data = jnp.concatenate([high, high, low], axis=0)
+        for start in (partner_half, own_half):
+            rows = pl.ds(start, outs // 2)
+            total[rows, :] += dot(weight_t[across_y, chunk, rows, :], data)
+            if start is partner_half:
+                to_partner.start()
 
     def gather(chunk):
         pltpu.make_async_copy(
@@ -414,17 +443,8 @@
 
     relay(CHUNKS - 1)
     finish(CHUNKS - 2)
-    finish(CHUNKS - 1)
-
-    to_partner = pltpu.make_async_remote_copy(
-        src_ref=total.at[pl.ds(partner_half, outs // 2), :],
-        dst_ref=partner_got,
-        send_sem=partner_send_sem,
-        recv_sem=partner_recv_sem,
-        device_id={"ch": partner},
-        device_id_type=MESH,
-    )
-    to_partner.start()
+    finish(CHUNKS - 1, final=True)
+
 
     @pl.loop(0, CHUNKS)
     def _(chunk):
@@ -466,6 +486,7 @@
             pltpu.VMEM((length, channels), f32),
             pltpu.VMEM((1, channels), f32),
             pltpu.VMEM((channels, length), f32),
+            pltpu.VMEM((slab // 8, 2 * parts * per_part, 2 * LANES), f32),
             pltpu.VMEM((2, channels * per_part, LANES), f32),
             pltpu.VMEM((2, CHUNKS, parts, slab, LANES), f32),
             pltpu.VMEM((CHUNKS, parts, slab, LANES), f32),

time: 61.9 us -> 61.7 us (level)
  no operation moved by 1% of the time
where the time goes in v2:
time: 61.7 us
  Pallas kernels  60.9 us (99%)
  local copies, waits for them, and re-layouts  0.8 us (1%)
    pallas_call x1, Pallas kernels, per_device(): pl.pallas_call(functools.partial(kernel, parts, ys), out_shape=pltpu.VMEM...  60.9 us

profile of v2, /device:TPU:1, one launch (start us, length us, event | category | flops | bytes accessed | tf_op | source)
XLA Modules:
  0.0 61.7 jit_solution(174412718397881434)
XLA Ops:
  0.0 60.9 %shard_map.154 = f32[256,512]{1,0:T(8,128)S(1)} custom-call(f32[512,256]{1,0:T(8,128)} %query_hbm.1, f32[512,256]{1,0:T(8,128)} %key_hbm.1, f32[512,256]{1,0:T(8,128)} %value_hbm.1, f32[512,256]{1,0:T(8,128)} %filter_hbm.1, f32[1,256]{1,0:T(1,128)} %bitcast.1, f32[256,2048]{1,0:T(8,128)} %weight_hbm.1, bf16[512,256]{1,0:T(8,128)(2,1)} %constant.20.clone.rest_0_, ...), custom_call_target="tpu_custom_call" | custom-call | tf_op jit(solution)/shard_map/pallas_call | solution.py:476
  60.9 0.8 %copy.18 = f32[256,512]{1,0:T(8,128)} copy(f32[256,512]{1,0:T(8,128)S(1)} %shard_map.154) | data formatting | bytes 1048576

commit v3 on v2

--- a/solution.py
+++ b/solution.py
@@ -97,7 +97,7 @@
     *rest,
 ):
     table_hbm, rest = rest[:10], rest[10:]
-    out_ref, rest = rest[0], rest[1:]
+    out_ref, partner_got, rest = rest[0], rest[1], rest[2:]
     table_ref, rest = rest[:10], rest[10:]
     (
         query_in,
@@ -115,7 +115,6 @@
         weight_t,
         mixed,
         total,
-        partner_got,
         load_sem,
         table_sem,
         send_sem,
@@ -192,27 +191,23 @@
     filter_in[0:1, :] = filter_in[0:1, :] + tap * skip_in[...]
 
     def send_chunk(chunk):
-        for which in (1, 0):
-
-            @pl.loop(1, parts)
-            def _(step):
-                peer = lax.rem(me + step, parts)
-                start = pl.multiple_of(chunk * parts * slab + peer * slab, slab)
-                pltpu.make_async_remote_copy(
-                    src_ref=sent.at[which, pl.ds(start, slab), :],
-                    dst_ref=got.at[which, chunk, me],
-                    send_sem=send_sem.at[which, chunk],
-                    recv_sem=recv_sem.at[which, chunk],
-                    device_id={"seq": peer},
-                    device_id_type=MESH,
-                ).start()
-
-            start = pl.multiple_of(chunk * parts * slab + me * slab, slab)
-            pltpu.make_async_copy(
-                sent.at[which, pl.ds(start, slab), :],
-                got.at[which, chunk, me],
-                recv_sem.at[which, chunk],
+        def slab_of(peer):
+            start = pl.multiple_of(chunk * parts * slab + peer * slab, slab)
+            return sent.at[:, pl.ds(start, slab), :]
+
+        @pl.loop(1, parts)
+        def _(step):
+            peer = lax.rem(me + step, parts)
+            pltpu.make_async_remote_copy(
+                src_ref=slab_of(peer),
+                dst_ref=got.at[:, chunk, me],
+                send_sem=send_sem.at[0, chunk],
+                recv_sem=recv_sem.at[0, chunk],
+                device_id={"seq": peer},
+                device_id_type=MESH,
             ).start()
+
+        pltpu.make_async_copy(slab_of(me), got.at[:, chunk, me], recv_sem.at[0, chunk]).start()
 
     def gated(rows, columns):
         return key_in[rows, columns] * value_in[rows, columns]
@@ -288,14 +283,14 @@
             data = got[which, chunk, :, rows, :].reshape(parts * 8, LANES)
             return spectrum(data, first, ahead, turn_cos[...], turn_sin[...])
 
-        arrived(1)
+        both = got.at[:, chunk]
+        pltpu.make_async_copy(both, both, recv_sem.at[0, chunk]).wait()
 
         @pl.loop(0, slab // 8)
         def _(pair):
             rows = pl.ds(pl.multiple_of(pair * 8, 8), 8)
             filter_spectrum[pair] = transformed(1, rows)
 
-        arrived(0)
 
         @pl.loop(0, slab // 8)
         def _(pair):
@@ -391,11 +386,11 @@
             return
         high, low = split(mixed[across_y, chunk])
         data = jnp.concatenate([high, high, low], axis=0)
-        for start in (partner_half, own_half):
-            rows = pl.ds(start, outs // 2)
-            total[rows, :] += dot(weight_t[across_y, chunk, rows, :], data)
-            if start is partner_half:
-                to_partner.start()
+        rows = pl.ds(partner_half, outs // 2)
+        total[rows, :] += dot(weight_t[across_y, chunk, rows, :], data)
+        to_partner.start()
+        rows = pl.ds(own_half, outs // 2)
+        out_ref[...] = total[rows, :] + dot(weight_t[across_y, chunk, rows, :], data)
 
     def gather(chunk):
         pltpu.make_async_copy(
@@ -448,9 +443,8 @@
 
     @pl.loop(0, CHUNKS)
     def _(chunk):
-        for which in range(2):
-            rest_of = got.at[which, chunk, pl.ds(0, parts - 1)]
-            pltpu.make_async_copy(rest_of, rest_of, send_sem.at[which, chunk]).wait()
+        rest_of = got.at[:, chunk, pl.ds(0, parts - 1)]
+        pltpu.make_async_copy(rest_of, rest_of, send_sem.at[0, chunk]).wait()
         rest_of = conv_sent.at[chunk, pl.ds(0, parts - 1)]
         pltpu.make_async_copy(rest_of, rest_of, conv_send_sem.at[chunk]).wait()
         for copy in own_copies(chunk) + relay_copies(chunk):
@@ -459,7 +453,6 @@
     for step in range(1, ys):
         weight_copy(step).wait_send()
     to_partner.wait()
-    out_ref[...] = total[pl.ds(own_half, outs // 2), :] + partner_got[...]
 
 
 def per_device(query_rows, key_rows, value_rows, filters, skip_gain, out_weight):
@@ -473,11 +466,11 @@
     consts = tables(parts, per_part)
     f32 = jnp.float32
     dma = pltpu.SemaphoreType.DMA
-    return pl.pallas_call(
+    own, other = pl.pallas_call(
         functools.partial(kernel, parts, ys),
-        out_shape=pltpu.VMEM((outs // 2, length), f32),
+        out_shape=[pltpu.VMEM((outs // 2, length), f32)] * 2,
         in_specs=[pl.BlockSpec(memory_space=pl.ANY)] * (6 + len(consts)),
-        out_specs=pl.BlockSpec(memory_space=pltpu.VMEM),
+        out_specs=[pl.BlockSpec(memory_space=pltpu.VMEM)] * 2,
         scratch_shapes=[
             *[pltpu.VMEM(table.shape, table.dtype) for table in consts],
             pltpu.VMEM((length, channels), f32),
@@ -495,7 +488,6 @@
             pltpu.VMEM((ys, CHUNKS, outs, 3 * chunk_channels), jnp.bfloat16),
             pltpu.VMEM((ys, CHUNKS, chunk_channels, length), f32),
             pltpu.VMEM((outs, length), f32),
-            pltpu.VMEM((outs // 2, length), f32),
             dma((5,)),
             dma((len(consts),)),
             dma((2, CHUNKS)),
@@ -519,6 +511,7 @@
         out_weight,
         *[jnp.asarray(table) for table in consts],
     )
+    return own + other
 
 
 def solution(mesh):

time: 61.7 us -> 61.7 us (level)
  other arithmetic: 0 us -> 0.87 us
  local copies, waits for them, and re-layouts: 0.8 us -> 0 us
    add x0 -> x1, other arithmetic: none -> 0.87 us  [per_device(): return own + other]
    unnamed x1 -> x0, local copies, waits for them, and re-layouts: 0.8 us -> none
where the time goes in v3:
time: 61.7 us
  Pallas kernels  60.8 us (99%)
  other arithmetic  0.87 us (1%)
    pallas_call x1, Pallas kernels, per_device(): pl.pallas_call(functools.partial(kernel, parts, ys), out_shape=[pltpu.VME...  60.8 us

profile of v3, /device:TPU:1, one launch (start us, length us, event | category | flops | bytes accessed | tf_op | source)
XLA Modules:
  0.0 61.7 jit_solution(1911569648209091138)
XLA Ops:
  0.0 60.8 %shard_map.154 = (f32[256,512]{1,0:T(8,128)S(1)}, f32[256,512]{1,0:T(8,128)S(1)}) custom-call(f32[512,256]{1,0:T(8,128)} %query_hbm.1, f32[512,256]{1,0:T(8,128)} %key_hbm.1, f32[512,256]{1,0:T(8,128)} %value_hbm.1, f32[512,256]{1,0:T(8,128)} %filter_hbm.1, f32[1,256]{1,0:T(1,128)} %bitcast.1, f32[256,2048]{1,0:T(8,128)} %weight_hbm.1, ...), custom_call_target="tpu_custom_call" | custom-call | tf_op jit(solution)/shard_map/pallas_call | solution.py:469
  60.8 0.9 %add.3 = f32[256,512]{1,0:T(8,128)} add(f32[256,512]{1,0:T(8,128)S(1)} %get-tuple-element.7, f32[256,512]{1,0:T(8,128)S(1)} %get-tuple-element.8) | non-fusion elementwise | flops 131072 | bytes 1572864 | tf_op jit(solution)/shard_map/add | solution.py:514

commit v4 on v3

--- a/solution.py
+++ b/solution.py
@@ -365,14 +365,17 @@
         mixed_copy(chunk, own_y, 1, False, 1).wait_recv()
         mixed_copy(chunk, ahead_y, 1, False, 5).start()
 
-    to_partner = pltpu.make_async_remote_copy(
-        src_ref=total.at[pl.ds(partner_half, outs // 2), :],
-        dst_ref=partner_got,
-        send_sem=partner_send_sem,
-        recv_sem=partner_recv_sem,
-        device_id={"ch": partner},
-        device_id_type=MESH,
-    )
+    quarter = outs // 4
+
+    def to_partner(part):
+        return pltpu.make_async_remote_copy(
+            src_ref=total.at[pl.ds(partner_half + part * quarter, quarter), :],
+            dst_ref=partner_got.at[pl.ds(part * quarter, quarter), :],
+            send_sem=partner_send_sem.at[part],
+            recv_sem=partner_recv_sem.at[part],
+            device_id={"ch": partner},
+            device_id_type=MESH,
+        )
 
     def finish(chunk, final=False):
         mixed_copy(chunk, own_y, 1, True, 2).wait_recv()
@@ -386,9 +389,10 @@
             return
         high, low = split(mixed[across_y, chunk])
         data = jnp.concatenate([high, high, low], axis=0)
-        rows = pl.ds(partner_half, outs // 2)
-        total[rows, :] += dot(weight_t[across_y, chunk, rows, :], data)
-        to_partner.start()
+        for part in range(2):
+            rows = pl.ds(partner_half + part * quarter, quarter)
+            total[rows, :] += dot(weight_t[across_y, chunk, rows, :], data)
+            to_partner(part).start()
         rows = pl.ds(own_half, outs // 2)
         out_ref[...] = total[rows, :] + dot(weight_t[across_y, chunk, rows, :], data)
 
@@ -452,7 +456,8 @@
 
     for step in range(1, ys):
         weight_copy(step).wait_send()
-    to_partner.wait()
+    for part in range(2):
+        to_partner(part).wait()
 
 
 def per_device(query_rows, key_rows, value_rows, filters, skip_gain, out_weight):
@@ -498,8 +503,8 @@
             dma((ys,)),
             dma((CHUNKS, 6)),
             dma((CHUNKS, 6)),
-            dma(()),
-            dma(()),
+            dma((2,)),
+            dma((2,)),
         ],
         compiler_params=pltpu.CompilerParams(collective_id=0, has_side_effects=True),
     )(

time: 61.7 us -> 61.7 us (level)
  no operation moved by 1% of the time
where the time goes in v4:
time: 61.7 us; the launch traced here: 61.6 us
  Pallas kernels  60.8 us (99%)
  other arithmetic  0.87 us (1%)
    pallas_call x1, Pallas kernels, per_device(): pl.pallas_call(functools.partial(kernel, parts, ys), out_shape=[pltpu.VME...  60.8 us

profile of v4, /device:TPU:1, one launch (start us, length us, event | category | flops | bytes accessed | tf_op | source)
XLA Modules:
  0.0 61.6 jit_solution(13004329760443538411)
XLA Ops:
  0.0 60.8 %shard_map.154 = (f32[256,512]{1,0:T(8,128)S(1)}, f32[256,512]{1,0:T(8,128)S(1)}) custom-call(f32[512,256]{1,0:T(8,128)} %query_hbm.1, f32[512,256]{1,0:T(8,128)} %key_hbm.1, f32[512,256]{1,0:T(8,128)} %value_hbm.1, f32[512,256]{1,0:T(8,128)} %filter_hbm.1, f32[1,256]{1,0:T(1,128)} %bitcast.1, f32[256,2048]{1,0:T(8,128)} %weight_hbm.1, ...), custom_call_target="tpu_custom_call" | custom-call | tf_op jit(solution)/shard_map/pallas_call | solution.py:474
  60.8 0.9 %add.3 = f32[256,512]{1,0:T(8,128)} add(f32[256,512]{1,0:T(8,128)S(1)} %get-tuple-element.7, f32[256,512]{1,0:T(8,128)S(1)} %get-tuple-element.8) | non-fusion elementwise | flops 131072 | bytes 1572864 | tf_op jit(solution)/shard_map/add | solution.py:519
